TPU v7x, 32 devices: a whole 2x2x4 slice. The times are simulated.
32 devices in a mesh: blk: 4 (over y, x), dp: 8 (over z, core).
Axes of the slice: x: 2, y: 2, z: 4, core: 2. Of those that a mesh axis runs over, the one named last changes fastest.
Arguments:
- embed: bfloat16 [8192, 768], P(('blk', 'dp')), may hold values from -0.23925781 to 0.23925781
- log_scale: float32 [1], replicated, may hold values from 3 to 3.7
- bias: float32 [1], replicated, may hold values from -5.5 to -3.5
- partner_count: int32 [8192], P(('blk', 'dp')), may hold values from 1 to 4, as said below
- partner_owner: int32 [8192, 4], P(('blk', 'dp')), may hold values from 0 to 31, as said below
- partner_row: int32 [8192, 4], P(('blk', 'dp')), may hold values from 0 to 255
Outputs:
- embed_grad: bfloat16 [8192, 768], P(('blk', 'dp'))
Inputs may be any that keep to these rules, and one draw needn't show every extreme that they name: `partner_count`: 4 on some row of every device. `partner_owner`: every entry names a device other than the row's own device (devices numbered index along blk times 8 plus index along dp). Among the first partner_count entries of the rows of one device, no device is named more than 34 times, and some device exactly 34 times.
All inputs are finite; a program needn't handle non-finite values.
Results may differ from a plain program's by a relative error of at most 0.0065.
Values may be sent and summed in bfloat16 or wider, within the bound.
A program may use at most 64 MiB of HBM per device.

v0:
```python
import math

import jax
import jax.numpy as jnp
from jax import lax
from jax.sharding import PartitionSpec as P


def body(embed, log_scale, bias, partner_count, partner_owner, partner_row):
    rows_here, width = embed.shape
    most = partner_owner.shape[1]
    values = embed.astype(jnp.float32)
    inv_norm = lax.rsqrt(jnp.mean(values * values, axis=1, keepdims=True) + 1e-06)
    root_width = 1.0 / math.sqrt(width)
    unit_rows = (values * inv_norm * root_width).astype(jnp.bfloat16)
    logit_scale = jnp.exp(log_scale[0])
    logit_bias = bias[0]
    my_start = lax.axis_index("blk") * rows_here
    row_ids = my_start + jnp.arange(rows_here, dtype=jnp.int32)
    group = lax.all_gather(unit_rows, "blk", axis=0, tiled=True)
    scores = lax.dot_general(
        unit_rows, group, (((1,), (1,)), ((), ())), preferred_element_type=jnp.float32
    )
    columns = jnp.arange(group.shape[0], dtype=jnp.int32)
    weights = jnp.where(
        row_ids[:, None] == columns[None, :],
        jnp.float32(0.0),
        jax.nn.sigmoid(logit_bias + logit_scale * scores),
    )
    summed = jnp.dot(weights.astype(jnp.bfloat16), group, preferred_element_type=jnp.float32)
    neg_grad = 2.0 * logit_scale * summed
    n_all = lax.axis_size(("blk", "dp"))
    capacity = -(-(rows_here * most) // (n_all - 1))
    slots_all = n_all * capacity
    owner_flat = partner_owner.reshape(-1)
    live = (jnp.arange(most, dtype=jnp.int32)[None, :] < partner_count[:, None]).reshape(-1)
    one_hot = (
        (owner_flat[:, None] == jnp.arange(n_all, dtype=jnp.int32)[None, :]) & live[:, None]
    ).astype(jnp.int32)
    earlier = jnp.cumsum(one_hot, axis=0) - one_hot
    rank_in = jnp.sum(earlier * one_hot, axis=1)
    slot_of = jnp.where(live, owner_flat * capacity + rank_in, slots_all)
    send_index = (
        jnp.zeros((slots_all,), jnp.int32).at[slot_of].set(partner_row.reshape(-1), mode="drop")
    )
    recv_index = lax.all_to_all(
        send_index.reshape(n_all, capacity), ("blk", "dp"), split_axis=0, concat_axis=0, tiled=True
    ).reshape(-1)
    safe_slot = jnp.minimum(slot_of, slots_all - 1)
    asking = jnp.broadcast_to(unit_rows[:, None, :], (rows_here, most, width)).reshape(-1, width)
    replies = unit_rows[recv_index].reshape(n_all, capacity, width)
    arrived = lax.all_to_all(
        replies, ("blk", "dp"), split_axis=0, concat_axis=0, tiled=True
    ).reshape(-1, width)
    partner = arrived[safe_slot]
    scores = jnp.einsum("nd,nd->n", asking, partner, preferred_element_type=jnp.float32)
    weight = jnp.where(live, jax.nn.sigmoid(-(logit_bias + logit_scale * scores)), jnp.float32(0.0))
    own_terms = (
        (-logit_scale * weight[:, None] * partner.astype(jnp.float32))
        .astype(jnp.bfloat16)
        .astype(jnp.float32)
    )
    back_terms = (-logit_scale * weight[:, None] * asking.astype(jnp.float32)).astype(jnp.bfloat16)
    outgoing = jnp.zeros((slots_all, width), jnp.bfloat16).at[slot_of].set(back_terms, mode="drop")
    received = lax.all_to_all(
        outgoing.reshape(n_all, capacity, width),
        ("blk", "dp"),
        split_axis=0,
        concat_axis=0,
        tiled=True,
    ).reshape(-1, width)
    incoming = jax.ops.segment_sum(received.astype(jnp.float32), recv_index, num_segments=rows_here)
    row_grad = neg_grad + jnp.sum(own_terms.reshape(rows_here, most, width), axis=1) + incoming
    inner = jnp.sum(values * row_grad, axis=1, keepdims=True)
    result = root_width * inv_norm * (row_grad - values * inv_norm * inv_norm * inner / width)
    return result.astype(jnp.bfloat16)


def solution(mesh):
    return jax.shard_map(
        body,
        mesh=mesh,
        in_specs=(
            P(("blk", "dp"), None),
            P(),
            P(),
            P(("blk", "dp")),
            P(("blk", "dp"), None),
            P(("blk", "dp"), None),
        ),
        out_specs=P(("blk", "dp"), None),
        check_vma=False,
    )
```

profile of v0, /device:TPU:1, one launch (start us, length us, event | category | flops | bytes accessed | tf_op | source)
XLA Modules:
  0.0 186.6 jit_solution(1436901027829189112)
XLA Ops:
  6.5 0.8 lt.85
  7.3 0.8 iota_compare_fusion.4
  8.1 0.8 copy.15
  9.5 0.7 broadcast_multiply_fusion
  10.5 9.0 %reduce-window.6 = s32[32,8,128]{2,1,0:T(8,128)S(1)} reduce-window(s32[32,8,128]{2,1,0:T(8,128)S(1)} %fusion.34, s32[]{:T(128)} %constant.21.clone.1), window={size=1x1x128 pad=0_0x0_0x127_0}, to_apply=%region_1.2 | reduce-window | flops 4161536 | bytes 262148 | tf_op jit(solution)/shard_map/reduce-window
  20.6 4.3 %scatter_custom_fusion = s32[1088]{0:T(1024)S(1)} fusion(s32[1024]{0:T(1024)S(1)} %bitcast.36, s32[1024]{0:T(1024)S(1)} %reshape.233, s32[]{:T(128)} %constant.21.clone.1), kind=kCustom, calls=%fused_computation.61 | custom fusion | bytes 4356 | tf_op jit(solution)/shard_map/scatter | solution.py:44
  24.9 0.7 all_to_all.12
  25.6 7.1 %all-to-all-start = ((s32[32,1,34]{2,1,0:T(1,128)}), s32[32,1,34]{2,1,0:T(1,128)S(1)}, u32[]{:S(2)}, u32[]{:S(2)}) async-start(s32[32,1,34]{2,1,0:T(1,128)} %all_to_all.12), calls=%async_computation | async-start | bytes 32768 | tf_op jit(solution)/shard_map/all_to_all | solution.py:46
  32.9 0.6 broadcast_multiply_fusion.1
  33.6 5.8 %all-to-all-done = s32[32,1,34]{2,1,0:T(1,128)S(1)} async-done(((s32[32,1,34]{2,1,0:T(1,128)}), s32[32,1,34]{2,1,0:T(1,128)S(1)}, u32[]{:S(2)}, u32[]{:S(2)}) %all-to-all-start) | async-done | bytes 4384 | tf_op jit(solution)/shard_map/all_to_all | solution.py:46
  39.5 0.6 broadcast.178
  40.1 0.7 reduce.9
  41.0 4.5 %gather_fusion = bf16[1088,768]{1,0:T(8,128)(2,1)S(1)} fusion(bf16[256,768]{1,0:T(8,128)(2,1)S(1)} %fusion.16, s32[2048]{0:T(1024)S(1)} %pad_clamp_fusion), kind=kCustom, calls=%fused_computation | custom fusion | bytes 3346688 | tf_op jit(solution)/shard_map/gather | solution.py:51
  45.5 1.5 reshape.208
  47.0 3.6 %all-to-all-start.1 = ((bf16[32,34,768]{2,1,0:T(8,128)(2,1)}), bf16[32,34,768]{2,1,0:T(8,128)(2,1)}, u32[]{:S(2)}, u32[]{:S(2)}) async-start(bf16[32,34,768]{2,1,0:T(8,128)(2,1)} %reshape.208), calls=%async_computation.1 | async-start | bytes 3932160 | tf_op jit(solution)/shard_map/all_to_all | solution.py:52
  52.8 44.8 %all-to-all-done.1 = bf16[32,34,768]{2,1,0:T(8,128)(2,1)} async-done(((bf16[32,34,768]{2,1,0:T(8,128)(2,1)}), bf16[32,34,768]{2,1,0:T(8,128)(2,1)}, u32[]{:S(2)}, u32[]{:S(2)}) %all-to-all-start.1) | async-done | bytes 1671200 | tf_op jit(solution)/shard_map/all_to_all | solution.py:52
  97.6 2.5 %reshape.209 = bf16[1088,768]{1,0:T(8,128)(2,1)S(1)} reshape(bf16[32,34,768]{2,1,0:T(8,128)(2,1)} %all-to-all-done.1) | data formatting | bytes 3342336 | tf_op jit(solution)/shard_map/reshape | solution.py:54
  100.1 5.2 %gather_fusion.1 = bf16[1024,768]{1,0:T(8,128)(2,1)} fusion(bf16[1088,768]{1,0:T(8,128)(2,1)S(1)} %reshape.209, s32[1024]{0:T(1024)S(1)} %broadcast_clamp_fusion), kind=kCustom, calls=%fused_computation.1 | custom fusion | bytes 3149824 | tf_op jit(solution)/shard_map/gather | solution.py:55
  105.3 1.9 %fusion = f32[1024]{0:T(1024)S(1)} fusion(bf16[1024,768]{1,0:T(8,128)(2,1)S(1)} %reshape.204, bf16[1024,768]{1,0:T(8,128)(2,1)} %gather_fusion.1), kind=kLoop, calls=%fused_computation.7 | loop fusion | flops 3144704 | bytes 3149824 | tf_op jit(solution)/shard_map/nd,nd->n/dot_general | solution.py:56
  107.2 6.1 %scatter_custom_fusion.1 = bf16[1088,768]{1,0:T(8,128)(2,1)S(1)} fusion(s32[1024]{0:T(1024)S(1)} %bitcast.37, bf16[1024,768]{1,0:T(8,128)(2,1)S(1)} %reshape.204, f32[1024]{0:T(1024)S(1)} %select_multiply_fusion, bf16[]{:T(256)} %constant.9.clone.1), kind=kCustom, calls=%fused_computation.11 | custom fusion | flops 2359296 | bytes 3248130 | tf_op jit(solution)/shard_map/scatter | solution.py:64
  113.3 1.5 reshape.210
  114.8 3.3 %all-to-all-start.2 = ((bf16[32,34,768]{2,1,0:T(8,128)(2,1)}), bf16[32,34,768]{2,1,0:T(8,128)(2,1)S(1)}, u32[]{:S(2)}, u32[]{:S(2)}) async-start(bf16[32,34,768]{2,1,0:T(8,128)(2,1)} %reshape.210), calls=%async_computation.2 | async-start | bytes 3932160 | tf_op jit(solution)/shard_map/all_to_all | solution.py:65
  119.4 0.7 reshape.247
  120.1 1.5 mul.150
  121.6 2.0 %reshape.211 = f32[256,4,768]{2,1,0:T(4,128)} reshape(bf16[1024,768]{1,0:T(8,128)(2,1)S(1)} %copy-done.2) | data formatting | bytes 4718592 | tf_op jit(solution)/shard_map/convert_element_type | solution.py:59
  123.6 4.8 %convert_reduce_fusion = f32[256,768]{1,0:T(8,128)} fusion(f32[256,4,768]{2,1,0:T(4,128)} %reshape.211, f32[256,4]{1,0:T(8,128)} %mul.150), kind=kLoop, calls=%fused_computation.9 | loop fusion | flops 2949120 | bytes 3936256 | tf_op jit(solution)/shard_map/reduce_sum | solution.py:73
  128.4 32.1 %all-gather.2.cloned.1.call-done = bf16[1024,768]{1,0:T(8,128)(2,1)} async-done(((bf16[256,768]{1,0:T(8,128)(2,1)}), bf16[1024,768]{1,0:T(8,128)(2,1)}) %all-gather.2.cloned.1.call-update) | async-done | bytes 1572880 | tf_op jit(solution)/shard_map/all_gather | solution.py:20
  160.6 3.3 %fusion.10 = f32[256,768]{1,0:T(8,128)S(1)} fusion(f32[256,768]{1,0:T(8,128)} %convert_reduce_fusion, bf16[1024,768]{1,0:T(8,128)(2,1)} %all-gather.2.cloned.1.call-done, bf16[256,768]{1,0:T(8,128)(2,1)S(1)} %copy-done.1, f32[]{:T(128)} %bitcast, f32[]{:T(128)} %bitcast.28, s32[256]{0:T(256)S(1)} %copy-done.11, f32[]{:T(128)S(6)} %mul_shard_map.3), kind=kOutput, calls=%fused_computation.20 | convolution fusion | flops 807796736 | bytes 3539980 | tf_op jit(solution)/shard_map/dot_general | solution.py:30
  163.9 1.1 all-to-all-done.2
  165.1 1.9 %reshape.249 = f32[1088,768]{1,0:T(8,128)} reshape(bf16[32,34,768]{2,1,0:T(8,128)(2,1)S(1)} %all-to-all-done.2) | data formatting | bytes 5013504 | tf_op jit(solution)/shard_map/convert_element_type | solution.py:72
  167.0 11.6 %scatter_fusion = f32[256,768]{1,0:T(8,128)S(1)} fusion(f32[256,768]{1,0:T(8,128)S(1)} %fusion.10, s32[1088]{0:T(1024)S(1)} %copy-done.6, f32[1088,768]{1,0:T(8,128)} %reshape.249), kind=kCustom, calls=%fused_computation.4 | custom fusion | flops 835584 | bytes 10031360 | tf_op jit(solution)/shard_map/scatter-add | solution.py:72
  178.7 1.0 fusion.21
  (60 shorter events, 4.6 us)
Async XLA Ops:
  6.5 13.7 %copy-start.9 = (s32[256,4]{0,1:T(4,128)S(1)}, s32[256,4]{0,1:T(4,128)}, u32[]{:S(2)}) copy-start(s32[256,4]{0,1:T(4,128)} %param.11) | copy-start | bytes 12292
  6.5 26.2 %copy-start.3 = (bf16[256,768]{1,0:T(8,128)(2,1)S(1)}, bf16[256,768]{1,0:T(8,128)(2,1)}, u32[]{:S(2)}) copy-start(bf16[256,768]{1,0:T(8,128)(2,1)} %param.6) | copy-start | bytes 1179652
  25.6 13.9 %all-to-all-start = ((s32[32,1,34]{2,1,0:T(1,128)}), s32[32,1,34]{2,1,0:T(1,128)S(1)}, u32[]{:S(2)}, u32[]{:S(2)}) async-start(s32[32,1,34]{2,1,0:T(1,128)} %all_to_all.12), calls=%async_computation | async-start | bytes 32768 | tf_op jit(solution)/shard_map/all_to_all | solution.py:46
  33.5 12.0 %copy-start.7 = (f32[256]{0:T(256)}, f32[256]{0:T(256)S(1)}, u32[]{:S(2)}) copy-start(f32[256]{0:T(256)S(1)} %get-tuple-element.8) | copy-start | bytes 3076
  33.6 17.0 %copy-start = (bf16[256,768]{1,0:T(8,128)(2,1)}, bf16[256,768]{1,0:T(8,128)(2,1)S(1)}, u32[]{:S(2)}) copy-start(bf16[256,768]{1,0:T(8,128)(2,1)S(1)} %fusion.16) | copy-start | bytes 1179652
  47.0 50.6 %all-to-all-start.1 = ((bf16[32,34,768]{2,1,0:T(8,128)(2,1)}), bf16[32,34,768]{2,1,0:T(8,128)(2,1)}, u32[]{:S(2)}, u32[]{:S(2)}) async-start(bf16[32,34,768]{2,1,0:T(8,128)(2,1)} %reshape.208), calls=%async_computation.1 | async-start | bytes 3932160 | tf_op jit(solution)/shard_map/all_to_all | solution.py:52
  107.2 6.1 %copy-start.5 = (f32[1024]{0:T(1024)}, f32[1024]{0:T(1024)S(1)}, u32[]{:S(2)}) copy-start(f32[1024]{0:T(1024)S(1)} %select_multiply_fusion) | copy-start | bytes 12292
  114.8 6.8 %copy-start.2 = (bf16[1024,768]{1,0:T(8,128)(2,1)S(1)}, bf16[1024,768]{1,0:T(8,128)(2,1)}, u32[]{:S(2)}) copy-start(bf16[1024,768]{1,0:T(8,128)(2,1)} %gather_fusion.1) | copy-start | bytes 4718596
  114.8 50.2 %all-to-all-start.2 = ((bf16[32,34,768]{2,1,0:T(8,128)(2,1)}), bf16[32,34,768]{2,1,0:T(8,128)(2,1)S(1)}, u32[]{:S(2)}, u32[]{:S(2)}) async-start(bf16[32,34,768]{2,1,0:T(8,128)(2,1)} %reshape.210), calls=%async_computation.2 | async-start | bytes 3932160 | tf_op jit(solution)/shard_map/all_to_all | solution.py:65
  118.2 42.4 %all-gather.2.cloned.1.call-start = ((), (), s32[]{:S(2)}) async-start(), calls=%async_computation.3 | async-start | bytes 1966080 | tf_op jit(solution)/shard_map/all_gather | solution.py:20
  123.6 36.9 %copy-start.1 = (bf16[256,768]{1,0:T(8,128)(2,1)S(1)}, bf16[256,768]{1,0:T(8,128)(2,1)}, u32[]{:S(2)}) copy-start(bf16[256,768]{1,0:T(8,128)(2,1)} %copy-done) | copy-start | bytes 1179652
  123.6 36.9 %copy-start.11 = (s32[256]{0:T(256)S(1)}, s32[256]{0:T(256)}, u32[]{:S(2)}) copy-start(s32[256]{0:T(256)} %iota_add_fusion) | copy-start | bytes 3076
  163.9 3.0 %copy-start.6 = (s32[1088]{0:T(1024)S(1)}, s32[1088]{0:T(1024)}, u32[]{:S(2)}) copy-start(s32[1088]{0:T(1024)} %reshape.247) | copy-start | bytes 13060
  167.0 11.6 %copy-start.4 = (bf16[256,768]{1,0:T(8,128)(2,1)S(1)}, bf16[256,768]{1,0:T(8,128)(2,1)}, u32[]{:S(2)}) copy-start(bf16[256,768]{1,0:T(8,128)(2,1)} %param.6) | copy-start | bytes 1179652
  167.0 11.8 %copy-start.8 = (f32[256]{0:T(256)S(1)}, f32[256]{0:T(256)}, u32[]{:S(2)}) copy-start(f32[256]{0:T(256)} %copy-done.7) | copy-start | bytes 3076
  167.0 11.8 %copy-start.10 = (f32[256]{0:T(256)S(1)}, f32[256]{0:T(256)}, u32[]{:S(2)}) copy-start(f32[256]{0:T(256)} %get-tuple-element.7) | copy-start | bytes 3076
Sparse Core Ops, SparseCore 0:
  120.8 39.6 all-gather.1
where the time goes:
time: 188 us; the launch traced here: 187 us
  waiting for transfers between devices  84.4 us (45%)
  other arithmetic  38.4 us (20%)
  local copies, waits for them, and re-layouts  31.1 us (17%)
  between operations  15.1 us (8%)
  starting transfers between devices  14.2 us (8%)
  matrix products  3.34 us (2%)
    all_to_all x1, waiting for transfers between devices, body(): lax.all_to_all(replies, ('blk', 'dp'), split_axis=0, concat_axis=0, tiled...  44.8 us
    all_gather x1, waiting for transfers between devices, body(): group = lax.all_gather(unit_rows, 'blk', axis=0, tiled=True)  32.1 us
    scatter-add x1, other arithmetic, body(): jax.ops.segment_sum(received.astype(jnp.float32), recv_index, num_segment...  11.6 us
    another operation x3, other arithmetic  9.15 us
    all_to_all x1, starting transfers between devices, body(): lax.all_to_all(send_index.reshape(n_all, capacity), ('blk', 'dp'), split_...  7.1 us
    scatter x1, other arithmetic, body(): jnp.zeros((slots_all, width), jnp.bfloat16).at[slot_of]  6.08 us
    all_to_all x1, waiting for transfers between devices, body(): lax.all_to_all(send_index.reshape(n_all, capacity), ('blk', 'dp'), split_...  5.83 us
    gather x1, local copies, waits for them, and re-layouts, body(): partner = arrived[safe_slot]  5.21 us
  transfers between devices with their start and end apart: 4, of which 4 were waited for; matrix products, arithmetic and copies ran while one was open for 8% of the time, Pallas kernels for 0%

commit v1 on v0

v1 whole, which is shorter than its diff:
```python
import functools
import math

import jax
import jax.numpy as jnp
from jax import lax
from jax.experimental import pallas as pl
from jax.experimental.pallas import tpu as pltpu
from jax.sharding import PartitionSpec as P

MESH = pl.DeviceIdType.MESH


def lookup(table, index):
    value = jnp.int32(table[0])
    for k in range(1, len(table)):
        value = jnp.where(index == k, jnp.int32(table[k]), value)
    return value


def kernel(
    n_blk, n_dp, log_scale_ref, bias_ref, x_ref, mine_ref, theirs_ref, o_ref,
    buf, keys, acc, wanted, z_sem, right_sem, left_sem, sib_sem, recv_sem, key_send, key_recv,
):
    rows, width = x_ref.shape
    most = mine_ref.shape[1]
    half = rows // 2
    n_all = n_blk * n_dp
    n_z = n_dp // 2
    far = n_blk // 2
    events = n_blk * n_z
    i, j = lax.axis_index("blk"), lax.axis_index("dp")
    z, c = j // 2, j % 2
    me = i * n_dp + j

    ring = [p ^ (p >> 1) for p in range(n_blk)]
    place = [ring.index(k) for k in range(n_blk)]
    pos = lookup(place, i)
    blk_at = lambda p: lookup(ring, lax.rem(p + n_blk, n_blk))
    right, left = blk_at(pos + 1), blk_at(pos - 1)
    order = []
    for a in range(n_z):
        order += sorted(range(n_z), key=lambda b: (abs(b - a), b))
    z_at = lambda t: lookup(order, z * n_z + t)
    slot = lambda bi, zz, cc: (bi * n_z + zz) * 2 + cc

    def copy(f, h, device, send, recv):
        if h is None:
            span = pl.ds(pl.multiple_of(f * rows, rows), rows)
        else:
            span = pl.ds(pl.multiple_of(f * rows + h * half, half), half)
        return pltpu.make_async_remote_copy(
            src_ref=buf.at[span], dst_ref=buf.at[span], send_sem=send, recv_sem=recv,
            device_id=device, device_id_type=MESH,
        )

    def to_right(f, h, e):
        return copy(f, h, (right, j), right_sem.at[e], recv_sem.at[f, h or 0])

    def to_left(f, h, e):
        return copy(f, h, (left, j), left_sem.at[e], recv_sem.at[f, h or 0])

    def to_sib(f, e):
        return copy(f, None, (i, z * 2 + 1 - c), sib_sem.at[e], recv_sem.at[f, 0])

    def to_z(t):
        return copy(me, None, (i, z_at(t) * 2 + c), z_sem.at[t], recv_sem.at[me, 0])

    def arrived(f, h):
        copy(f, h, (right, j), right_sem.at[0], recv_sem.at[f, h or 0]).wait_recv()

    def place_of(e):
        t, m = e // n_blk, e % n_blk
        d = (m + 1) // 2
        return t, m, d, blk_at(jnp.where(m % 2 == 1, pos - d, pos + d)), z_at(t)

    barrier = pltpu.get_barrier_semaphore()

    @pl.loop(1, n_all)
    def _(k):
        f = lax.rem(me + k, n_all)
        pl.semaphore_signal(barrier, 1, device_id=(f // n_dp, f % n_dp), device_id_type=MESH)

    root = 1.0 / math.sqrt(width)
    x = x_ref[...].astype(jnp.float32)
    inv = lax.rsqrt(jnp.mean(x * x, axis=1, keepdims=True) + 1e-06)
    own = pl.ds(pl.multiple_of(me * rows, rows), rows)
    buf[own, :] = (x * inv * root).astype(jnp.bfloat16)
    keys[pl.ds(me, 1)] = theirs_ref[...]
    pl.semaphore_wait(barrier, n_all - 1)

    to_right(me, None, 0).start()
    to_left(me, None, 0).start()
    for t in range(1, n_z):
        to_z(t).start()
    to_sib(me, 0).start()

    def key_copy(src, dst, f):
        return pltpu.make_async_remote_copy(
            src_ref=src, dst_ref=dst, send_sem=key_send, recv_sem=key_recv,
            device_id=(f // n_dp, f % n_dp), device_id_type=MESH,
        )

    @pl.loop(1, n_all)
    def _(k):
        f = lax.rem(me + k, n_all)
        key_copy(theirs_ref, keys.at[pl.ds(me, 1)], f).start()

    acc[...] = jnp.zeros_like(acc)
    for k in range(most):
        wanted[k] = jnp.broadcast_to(mine_ref[:, k : k + 1], (rows, 128))
    scale = jnp.exp(jnp.full((1, 1), log_scale_ref[0], jnp.float32))
    offset = jnp.full((1, 1), bias_ref[0], jnp.float32)
    everything = keys.at[pl.ds(0, n_all - 1)]
    key_copy(everything, everything, lax.rem(me + 1, n_all)).wait()

    def compute(e):
        _, _, _, bi, zz = place_of(e)
        arrived(slot(bi, zz, 1 - c), None)
        pair = bi * n_z + zz
        start = pair * 2 * rows
        block = buf[pl.ds(pl.multiple_of(start, 2 * rows), 2 * rows), :]
        scores = lax.dot_general(
            buf[own, :], block, (((1,), (1,)), ((), ())), preferred_element_type=jnp.float32
        )
        lanes = lax.broadcasted_iota(jnp.int32, (rows, 128), 1)
        here = lax.broadcasted_iota(jnp.int32, (rows, 128), 0) + me * rows
        weights = []
        for u in range(2 * rows // 128):
            side, at = u * 128 // rows, u * 128 % rows
            columns = lanes + (start + u * 128)
            named = jnp.zeros((rows, 128), jnp.float32)
            for k in range(most):
                named += jnp.where(wanted[k] == columns, 1.0, 0.0)
            for k in range(most):
                key = keys[pair * 2 + side, k : k + 1, at : at + 128]
                named += jnp.where(key == here, 1.0, 0.0)
            power = jnp.exp(offset + scale * scores[:, u * 128 : (u + 1) * 128])
            gain = jnp.where(jnp.logical_and(zz == z, c == side), 2.0, 0.0)
            negative = jnp.where(columns == here, 0.0, gain * power)
            weights.append(((negative - named) / (1.0 + power)).astype(jnp.bfloat16))
        weight = jnp.concatenate(weights, axis=1)
        acc[...] += jnp.dot(weight, block, preferred_element_type=jnp.float32)

    @pl.loop(0, events)
    def _(e):
        t, m, d, bi, zz = place_of(e)

        @pl.when(jnp.logical_and(m == 0, t + 1 < n_z))
        def _():
            f = slot(i, z_at(t + 1), c)
            arrived(f, None)
            to_right(f, None, e + n_blk).start()
            to_left(f, None, e + n_blk).start()
            to_sib(f, e + n_blk).start()

        f = slot(bi, zz, c)

        @pl.when(jnp.logical_and(m > 0, m < n_blk - 1))
        def _():
            arrived(f, None)

        for parity, send in ((1, to_right), (0, to_left)):
            mine = jnp.logical_and(jnp.logical_and(m > 0, m < n_blk - 1), m % 2 == parity)

            @pl.when(jnp.logical_and(mine, d == far - 1))
            def _():
                send(f, 1 - parity, e).start()

            if far > 2:
                @pl.when(jnp.logical_and(mine, d < far - 1))
                def _():
                    send(f, None, e).start()

        @pl.when(m == n_blk - 1)
        def _():
            arrived(f, 0)
            arrived(f, 1)

        @pl.when(m > 0)
        def _():
            to_sib(f, e).start()

        @pl.when(e > 0)
        def _():
            compute(e - 1)

    compute(events - 1)

    t_acc = scale * acc[...]
    x = x_ref[...].astype(jnp.float32)
    inv = lax.rsqrt(jnp.mean(x * x, axis=1, keepdims=True) + 1e-06)
    inner = jnp.sum(x * t_acc, axis=1, keepdims=True)
    o_ref[...] = (root * inv * (t_acc - x * (inv * inv * inner / width))).astype(o_ref.dtype)

    for t in range(1, n_z):
        to_z(t).wait_send()

    @pl.loop(0, events)
    def _(e):
        t, m, d, bi, zz = place_of(e)
        f = slot(bi, zz, c)
        to_sib(f, e).wait_send()

        @pl.when(m == 0)
        def _():
            to_right(f, None, e).wait_send()
            to_left(f, None, e).wait_send()

        for parity, send in ((1, to_right), (0, to_left)):
            mine = jnp.logical_and(jnp.logical_and(m > 0, m < n_blk - 1), m % 2 == parity)

            @pl.when(jnp.logical_and(mine, d == far - 1))
            def _():
                send(f, 1 - parity, e).wait_send()

            if far > 2:
                @pl.when(jnp.logical_and(mine, d < far - 1))
                def _():
                    send(f, None, e).wait_send()


def body(n_blk, n_dp, embed, log_scale, bias, partner_count, partner_owner, partner_row):
    rows, width = embed.shape
    most = partner_owner.shape[1]
    n_all = n_blk * n_dp
    events = n_all // 2
    live = jnp.arange(most, dtype=jnp.int32)[None, :] < partner_count[:, None]
    mine = jnp.where(live, partner_owner * rows + partner_row, -1)
    theirs = mine.T.reshape(1, most, rows)
    vmem = pl.BlockSpec(memory_space=pltpu.VMEM)
    smem = pl.BlockSpec(memory_space=pltpu.SMEM)
    return pl.pallas_call(
        functools.partial(kernel, n_blk, n_dp),
        out_shape=jax.ShapeDtypeStruct((rows, width), embed.dtype),
        in_specs=[smem, smem, vmem, vmem, vmem],
        out_specs=vmem,
        scratch_shapes=[
            pltpu.VMEM((n_all * rows, width), jnp.bfloat16),
            pltpu.VMEM((n_all, most, rows), jnp.int32),
            pltpu.VMEM((rows, width), jnp.float32),
            pltpu.VMEM((most, rows, 128), jnp.int32),
            pltpu.SemaphoreType.DMA((n_dp // 2,)),
            pltpu.SemaphoreType.DMA((events,)),
            pltpu.SemaphoreType.DMA((events,)),
            pltpu.SemaphoreType.DMA((events,)),
            pltpu.SemaphoreType.DMA((n_all, 2)),
            pltpu.SemaphoreType.DMA,
            pltpu.SemaphoreType.DMA,
        ],
        compiler_params=pltpu.CompilerParams(
            collective_id=0, has_side_effects=True, vmem_limit_bytes=60 * 1024 * 1024
        ),
    )(log_scale, bias, embed, mine, theirs)


def solution(mesh):
    return jax.shard_map(
        functools.partial(body, mesh.shape["blk"], mesh.shape["dp"]),
        mesh=mesh,
        in_specs=(
            P(("blk", "dp"), None),
            P(),
            P(),
            P(("blk", "dp")),
            P(("blk", "dp"), None),
            P(("blk", "dp"), None),
        ),
        out_specs=P(("blk", "dp"), None),
        check_vma=False,
    )
```

time: 188 us -> 111 us (0.59)
  Pallas kernels: 0 us -> 106 us
  waiting for transfers between devices: 84.4 us -> 0 us
  other arithmetic: 38.4 us -> 0.71 us
  local copies, waits for them, and re-layouts: 31.1 us -> 2.58 us
  starting transfers between devices: 14.2 us -> 0 us
  between operations: 15.1 us -> 1.33 us
  matrix products: 3.34 us -> 0 us
    pallas_call x0 -> x1, Pallas kernels: none -> 106 us  [body(): pl.pallas_call(functools.partial(kernel, n_blk, n_dp), out_shape=jax.Shap...]
    all_to_all x3 -> x0, waiting for transfers between devices: 51.7 us -> none  [the longest x1 44.8 us: body(): lax.all_to_all(replies, ('blk', 'dp'), split_axis=0, concat_axis=0, tiled...]
    all_gather x1 -> x0, waiting for transfers between devices: 32.1 us -> none  [body(): group = lax.all_gather(unit_rows, 'blk', axis=0, tiled=True)]
    all_to_all x3 -> x0, starting transfers between devices: 14 us -> none  [the longest x1 7.1 us: body(): lax.all_to_all(send_index.reshape(n_all, capacity), ('blk', 'dp'), split_...]
    scatter-add x1 -> x0, other arithmetic: 11.6 us -> none  [body(): jax.ops.segment_sum(received.astype(jnp.float32), recv_index, num_segment...]
    gather x2 -> x0, local copies, waits for them, and re-layouts: 9.72 us -> none  [the longest x1 5.21 us: body(): partner = arrived[safe_slot]]
    another operation x3 -> x0, other arithmetic: 9.15 us -> none
    reshape x7 -> x0, local copies, waits for them, and re-layouts: 6.87 us -> none  [the longest x1 2.48 us: body(): arrived = lax.all_to_all(replies, ('blk', 'dp'), split_axis=0, concat_axi...]
  transfers between devices with their start and end apart: 4 -> 0, of which waited for: 4 -> 0; matrix products, arithmetic and copies ran while one was open for 8% -> 0% of each run, Pallas kernels for 0% -> 0%
where the time goes in v1:
time: 111 us
  Pallas kernels  106 us (95%)
  local copies, waits for them, and re-layouts  2.58 us (2%)
  between operations  1.33 us (1%)
    pallas_call x1, Pallas kernels, body(): pl.pallas_call(functools.partial(kernel, n_blk, n_dp), out_shape=jax.Shap...  106 us

profile of v1, /device:TPU:1, one launch (start us, length us, event | category | flops | bytes accessed | tf_op | source)
XLA Modules:
  0.0 110.7 jit_solution(10027547121067033901)
XLA Ops:
  0.7 0.0 copy-start.1
  1.3 0.0 copy-done.1
  1.3 0.7 add_select_fusion
  2.0 0.0 copy-start
  2.0 0.8 copy.7.mine_ref
  2.8 0.0 copy-done
  2.8 106.0 %shard_map.64 = bf16[256,768]{1,0:T(8,128)(2,1)} custom-call(f32[1]{0:T(128)S(6)} %copy.9.log_scale_ref, f32[1]{0:T(128)S(6)} %copy.10.bias_ref, bf16[256,768]{1,0:T(8,128)(2,1)} %x_ref.1, s32[256,4]{1,0:T(8,128)} %copy.7.mine_ref, s32[1,4,256]{2,1,0:T(4,128)} %bitcast.3), custom_call_target="tpu_custom_call" | custom-call | tf_op jit(solution)/shard_map/pallas_call | solution.py:233
  108.9 1.8 %copy.11 = bf16[256,768]{1,0:T(8,128)(2,1)} copy(bf16[256,768]{1,0:T(8,128)(2,1)} %shard_map.64) | data formatting | bytes 786432
Async XLA Ops:
  0.7 0.7 copy-start.1
  2.0 0.8 copy-start

commit v2 on v1

--- a/solution.py
+++ b/solution.py
@@ -63,14 +63,16 @@
     def to_sib(f, e):
         return copy(f, None, (i, z * 2 + 1 - c), sib_sem.at[e], recv_sem.at[f, 0])
 
-    def to_z(t):
-        return copy(me, None, (i, z_at(t) * 2 + c), z_sem.at[t], recv_sem.at[me, 0])
+    def along_z(zz, step, k):
+        f = slot(i, zz, c)
+        return copy(f, None, (i, (z + step) * 2 + c), z_sem.at[zz, k], recv_sem.at[f, 0])
 
     def arrived(f, h):
         copy(f, h, (right, j), right_sem.at[0], recv_sem.at[f, h or 0]).wait_recv()
 
     def place_of(e):
         t, m = e // n_blk, e % n_blk
+        t = jnp.where(m == n_blk - 1, t - 1, t)
         d = (m + 1) // 2
         return t, m, d, blk_at(jnp.where(m % 2 == 1, pos - d, pos + d)), z_at(t)
 
@@ -89,11 +91,18 @@
     keys[pl.ds(me, 1)] = theirs_ref[...]
     pl.semaphore_wait(barrier, n_all - 1)
 
-    to_right(me, None, 0).start()
-    to_left(me, None, 0).start()
-    for t in range(1, n_z):
-        to_z(t).start()
-    to_sib(me, 0).start()
+    to_right(me, None, z).start()
+    to_left(me, None, z).start()
+
+    @pl.when(z < n_z - 1)
+    def _():
+        along_z(z, 1, 0).start()
+
+    @pl.when(z > 0)
+    def _():
+        along_z(z, -1, 1).start()
+
+    to_sib(me, z).start()
 
     def key_copy(src, dst, f):
         return pltpu.make_async_remote_copy(
@@ -142,50 +151,62 @@
         weight = jnp.concatenate(weights, axis=1)
         acc[...] += jnp.dot(weight, block, preferred_element_type=jnp.float32)
 
-    @pl.loop(0, events)
+    @pl.loop(0, events + n_blk)
     def _(e):
         t, m, d, bi, zz = place_of(e)
-
-        @pl.when(jnp.logical_and(m == 0, t + 1 < n_z))
-        def _():
-            f = slot(i, z_at(t + 1), c)
+        valid = jnp.logical_and(t >= 0, t < n_z)
+
+        for step, k in ((1, 1), (-1, 0)):
+            origin = z + step * (t + 1)
+
+            @pl.when(jnp.logical_and(m == 0, jnp.logical_and(origin >= 0, origin < n_z)))
+            def _():
+                f = slot(i, origin, c)
+                arrived(f, None)
+
+                @pl.when(jnp.logical_and(z - step >= 0, z - step < n_z))
+                def _():
+                    along_z(origin, -step, k).start()
+
+                to_right(f, None, origin).start()
+                to_left(f, None, origin).start()
+                to_sib(f, origin).start()
+
+        f = slot(bi, zz, c)
+        passing = jnp.logical_and(valid, jnp.logical_and(m > 0, m < n_blk - 1))
+
+        @pl.when(passing)
+        def _():
             arrived(f, None)
-            to_right(f, None, e + n_blk).start()
-            to_left(f, None, e + n_blk).start()
-            to_sib(f, e + n_blk).start()
-
-        f = slot(bi, zz, c)
-
-        @pl.when(jnp.logical_and(m > 0, m < n_blk - 1))
-        def _():
-            arrived(f, None)
 
         for parity, send in ((1, to_right), (0, to_left)):
-            mine = jnp.logical_and(jnp.logical_and(m > 0, m < n_blk - 1), m % 2 == parity)
+            mine = jnp.logical_and(passing, m % 2 == parity)
 
             @pl.when(jnp.logical_and(mine, d == far - 1))
             def _():
-                send(f, 1 - parity, e).start()
+                send(f, 1 - parity, m * n_z + zz).start()
 
             if far > 2:
                 @pl.when(jnp.logical_and(mine, d < far - 1))
                 def _():
-                    send(f, None, e).start()
-
-        @pl.when(m == n_blk - 1)
+                    send(f, None, m * n_z + zz).start()
+
+        @pl.when(jnp.logical_and(valid, m == n_blk - 1))
         def _():
             arrived(f, 0)
             arrived(f, 1)
 
-        @pl.when(m > 0)
-        def _():
-            to_sib(f, e).start()
-
-        @pl.when(e > 0)
+        @pl.when(jnp.logical_and(valid, m > 0))
+        def _():
+            to_sib(f, m * n_z + zz).start()
+
+        before = place_of(e - 1 + n_blk)[0] - 1
+
+        @pl.when(jnp.logical_and(e > 0, jnp.logical_and(before >= 0, before < n_z)))
         def _():
             compute(e - 1)
 
-    compute(events - 1)
+    compute(events + n_blk - 1)
 
     t_acc = scale * acc[...]
     x = x_ref[...].astype(jnp.float32)
@@ -193,31 +214,38 @@
     inner = jnp.sum(x * t_acc, axis=1, keepdims=True)
     o_ref[...] = (root * inv * (t_acc - x * (inv * inv * inner / width))).astype(o_ref.dtype)
 
-    for t in range(1, n_z):
-        to_z(t).wait_send()
+    @pl.loop(0, n_z)
+    def _(zz):
+        @pl.when(jnp.logical_and(zz <= z, z < n_z - 1))
+        def _():
+            along_z(zz, 1, 0).wait_send()
+
+        @pl.when(jnp.logical_and(zz >= z, z > 0))
+        def _():
+            along_z(zz, -1, 1).wait_send()
 
     @pl.loop(0, events)
     def _(e):
-        t, m, d, bi, zz = place_of(e)
-        f = slot(bi, zz, c)
-        to_sib(f, e).wait_send()
+        m, zz = e // n_z, e % n_z
+        to_sib(me, e).wait_send()
 
         @pl.when(m == 0)
         def _():
-            to_right(f, None, e).wait_send()
-            to_left(f, None, e).wait_send()
-
+            to_right(me, None, e).wait_send()
+            to_left(me, None, e).wait_send()
+
+        passing = jnp.logical_and(m > 0, m < n_blk - 1)
         for parity, send in ((1, to_right), (0, to_left)):
-            mine = jnp.logical_and(jnp.logical_and(m > 0, m < n_blk - 1), m % 2 == parity)
-
-            @pl.when(jnp.logical_and(mine, d == far - 1))
+            mine = jnp.logical_and(passing, m % 2 == parity)
+
+            @pl.when(jnp.logical_and(mine, (m + 1) // 2 == far - 1))
             def _():
-                send(f, 1 - parity, e).wait_send()
+                send(me, 0, e).wait_send()
 
             if far > 2:
-                @pl.when(jnp.logical_and(mine, d < far - 1))
+                @pl.when(jnp.logical_and(mine, (m + 1) // 2 < far - 1))
                 def _():
-                    send(f, None, e).wait_send()
+                    send(me, None, e).wait_send()
 
 
 def body(n_blk, n_dp, embed, log_scale, bias, partner_count, partner_owner, partner_row):
@@ -240,7 +268,7 @@
             pltpu.VMEM((n_all, most, rows), jnp.int32),
             pltpu.VMEM((rows, width), jnp.float32),
             pltpu.VMEM((most, rows, 128), jnp.int32),
-            pltpu.SemaphoreType.DMA((n_dp // 2,)),
+            pltpu.SemaphoreType.DMA((n_dp // 2, 2)),
             pltpu.SemaphoreType.DMA((events,)),
             pltpu.SemaphoreType.DMA((events,)),
             pltpu.SemaphoreType.DMA((events,)),

time: 111 us -> 76 us (0.68)
  Pallas kernels: 106 us -> 70 us
    pallas_call x1, Pallas kernels: 106 us -> 70 us  [body(): pl.pallas_call(functools.partial(kernel, n_blk, n_dp), out_shape=jax.Shap...]
where the time goes in v2:
time: 76 us; the launch traced here: 74.6 us
  Pallas kernels  70 us (92%)
  local copies, waits for them, and re-layouts  2.58 us (3%)
  between operations  1.33 us (2%)
    pallas_call x1, Pallas kernels, body(): pl.pallas_call(functools.partial(kernel, n_blk, n_dp), out_shape=jax.Shap...  70 us
    unnamed x5, local copies, waits for them, and re-layouts  1.78 us

profile of v2, /device:TPU:1, one launch (start us, length us, event | category | flops | bytes accessed | tf_op | source)
XLA Modules:
  0.0 74.6 jit_solution(8488078489095609376)
XLA Ops:
  0.7 0.0 copy-start.1
  1.3 0.0 copy-done.1
  1.3 0.7 add_select_fusion
  2.0 0.0 copy-start
  2.0 0.8 %copy.7.mine_ref = s32[256,4]{1,0:T(8,128)} copy(s32[256,4]{0,1:T(4,128)S(1)} %add_select_fusion) | data formatting | bytes 8192 | tf_op jit(solution)/shard_map/jit(_where)/select_n | solution.py:257
  2.8 0.0 copy-done
  2.8 70.0 %shard_map.64 = bf16[256,768]{1,0:T(8,128)(2,1)} custom-call(f32[1]{0:T(128)S(6)} %copy.9.log_scale_ref, f32[1]{0:T(128)S(6)} %copy.10.bias_ref, bf16[256,768]{1,0:T(8,128)(2,1)} %x_ref.1, s32[256,4]{1,0:T(8,128)} %copy.7.mine_ref, s32[1,4,256]{2,1,0:T(4,128)} %bitcast.3), custom_call_target="tpu_custom_call" | custom-call | tf_op jit(solution)/shard_map/pallas_call | solution.py:261
  72.9 1.8 %copy.11 = bf16[256,768]{1,0:T(8,128)(2,1)} copy(bf16[256,768]{1,0:T(8,128)(2,1)} %shard_map.64) | data formatting | bytes 786432
Async XLA Ops:
  0.7 0.7 copy-start.1
  2.0 0.8 %copy-start = (s32[256,4]{0,1:T(4,128)}, s32[256,4]{0,1:T(4,128)S(1)}, u32[]{:S(2)}) copy-start(s32[256,4]{0,1:T(4,128)S(1)} %add_select_fusion) | copy-start | bytes 12292

commit v3 on v2

--- a/solution.py
+++ b/solution.py
@@ -19,11 +19,11 @@
 
 
 def kernel(
-    n_blk, n_dp, log_scale_ref, bias_ref, x_ref, mine_ref, theirs_ref, o_ref,
+    n_blk, n_dp, log_scale_ref, bias_ref, x_ref, theirs_ref, o_ref,
     buf, keys, acc, wanted, z_sem, right_sem, left_sem, sib_sem, recv_sem, key_send, key_recv,
 ):
     rows, width = x_ref.shape
-    most = mine_ref.shape[1]
+    most = theirs_ref.shape[1]
     half = rows // 2
     n_all = n_blk * n_dp
     n_z = n_dp // 2
@@ -67,6 +67,18 @@
         f = slot(i, zz, c)
         return copy(f, None, (i, (z + step) * 2 + c), z_sem.at[zz, k], recv_sem.at[f, 0])
 
+    far_blk = blk_at(pos + far)
+
+    def far_along_z(zz, step, k):
+        f = slot(far_blk, zz, c)
+        return copy(f, None, (i, (z + step) * 2 + c), z_sem.at[zz, 2 + k], recv_sem.at[f, 0])
+
+    def reach(zz):
+        return jnp.where(jnp.logical_and(zz >= 0, zz < n_z), 1, 0)
+
+    def halves(zz):
+        return jnp.logical_or(zz == z, jnp.maximum(zz - z, z - zz) > reach(z))
+
     def arrived(f, h):
         copy(f, h, (right, j), right_sem.at[0], recv_sem.at[f, h or 0]).wait_recv()
 
@@ -117,11 +129,10 @@
 
     acc[...] = jnp.zeros_like(acc)
     for k in range(most):
-        wanted[k] = jnp.broadcast_to(mine_ref[:, k : k + 1], (rows, 128))
+        wanted[k] = jnp.broadcast_to(theirs_ref[0, k : k + 1, :], (128, rows)).T
     scale = jnp.exp(jnp.full((1, 1), log_scale_ref[0], jnp.float32))
     offset = jnp.full((1, 1), bias_ref[0], jnp.float32)
     everything = keys.at[pl.ds(0, n_all - 1)]
-    key_copy(everything, everything, lax.rem(me + 1, n_all)).wait()
 
     def compute(e):
         _, _, _, bi, zz = place_of(e)
@@ -182,7 +193,7 @@
         for parity, send in ((1, to_right), (0, to_left)):
             mine = jnp.logical_and(passing, m % 2 == parity)
 
-            @pl.when(jnp.logical_and(mine, d == far - 1))
+            @pl.when(jnp.logical_and(jnp.logical_and(mine, halves(zz)), d == far - 1))
             def _():
                 send(f, 1 - parity, m * n_z + zz).start()
 
@@ -191,14 +202,43 @@
                 def _():
                     send(f, None, m * n_z + zz).start()
 
-        @pl.when(jnp.logical_and(valid, m == n_blk - 1))
-        def _():
-            arrived(f, 0)
-            arrived(f, 1)
-
-        @pl.when(jnp.logical_and(valid, m > 0))
+        @pl.when(jnp.logical_and(passing, m > 0))
         def _():
             to_sib(f, m * n_z + zz).start()
+
+        for step, k in ((1, 1), (-1, 0)):
+            origin = z + step * t
+            here = jnp.logical_and(origin >= 0, origin < n_z)
+            here = jnp.logical_and(here, jnp.logical_and(m == n_blk - 1, valid))
+            if step < 0:
+                here = jnp.logical_and(here, t > 0)
+
+            @pl.when(here)
+            def _():
+                g = slot(far_blk, origin, c)
+
+                @pl.when(halves(origin))
+                def _():
+                    arrived(g, 0)
+                    arrived(g, 1)
+
+                @pl.when(jnp.logical_not(halves(origin)))
+                def _():
+                    arrived(g, None)
+
+                @pl.when(t + 1 <= reach(z - step))
+                def _():
+                    far_along_z(origin, -step, k).start()
+
+                @pl.when(jnp.logical_and(t == 0, 1 <= reach(z + step)))
+                def _():
+                    far_along_z(origin, step, 1 - k).start()
+
+                to_sib(g, (n_blk - 1) * n_z + origin).start()
+
+        @pl.when(e == 1)
+        def _():
+            key_copy(everything, everything, lax.rem(me + 1, n_all)).wait()
 
         before = place_of(e - 1 + n_blk)[0] - 1
 
@@ -224,6 +264,14 @@
         def _():
             along_z(zz, -1, 1).wait_send()
 
+        @pl.when(jnp.logical_and(zz <= z, z + 1 - zz <= reach(z + 1)))
+        def _():
+            far_along_z(zz, 1, 0).wait_send()
+
+        @pl.when(jnp.logical_and(zz >= z, zz - z + 1 <= reach(z - 1)))
+        def _():
+            far_along_z(zz, -1, 1).wait_send()
+
     @pl.loop(0, events)
     def _(e):
         m, zz = e // n_z, e % n_z
@@ -238,7 +286,7 @@
         for parity, send in ((1, to_right), (0, to_left)):
             mine = jnp.logical_and(passing, m % 2 == parity)
 
-            @pl.when(jnp.logical_and(mine, (m + 1) // 2 == far - 1))
+            @pl.when(jnp.logical_and(jnp.logical_and(mine, halves(zz)), (m + 1) // 2 == far - 1))
             def _():
                 send(me, 0, e).wait_send()
 
@@ -253,22 +301,21 @@
     most = partner_owner.shape[1]
     n_all = n_blk * n_dp
     events = n_all // 2
-    live = jnp.arange(most, dtype=jnp.int32)[None, :] < partner_count[:, None]
-    mine = jnp.where(live, partner_owner * rows + partner_row, -1)
-    theirs = mine.T.reshape(1, most, rows)
+    live = jnp.arange(most, dtype=jnp.int32)[:, None] < partner_count[None, :]
+    theirs = jnp.where(live, partner_owner.T * rows + partner_row.T, -1).reshape(1, most, rows)
     vmem = pl.BlockSpec(memory_space=pltpu.VMEM)
     smem = pl.BlockSpec(memory_space=pltpu.SMEM)
     return pl.pallas_call(
         functools.partial(kernel, n_blk, n_dp),
         out_shape=jax.ShapeDtypeStruct((rows, width), embed.dtype),
-        in_specs=[smem, smem, vmem, vmem, vmem],
+        in_specs=[smem, smem, vmem, vmem],
         out_specs=vmem,
         scratch_shapes=[
             pltpu.VMEM((n_all * rows, width), jnp.bfloat16),
             pltpu.VMEM((n_all, most, rows), jnp.int32),
             pltpu.VMEM((rows, width), jnp.float32),
             pltpu.VMEM((most, rows, 128), jnp.int32),
-            pltpu.SemaphoreType.DMA((n_dp // 2, 2)),
+            pltpu.SemaphoreType.DMA((n_dp // 2, 4)),
             pltpu.SemaphoreType.DMA((events,)),
             pltpu.SemaphoreType.DMA((events,)),
             pltpu.SemaphoreType.DMA((events,)),
@@ -279,7 +326,7 @@
         compiler_params=pltpu.CompilerParams(
             collective_id=0, has_side_effects=True, vmem_limit_bytes=60 * 1024 * 1024
         ),
-    )(log_scale, bias, embed, mine, theirs)
+    )(log_scale, bias, embed, theirs)
 
 
 def solution(mesh):

time: 76 us -> 71.7 us (0.943); the launches traced: 74.6 us -> 71.4 us
  Pallas kernels: 70 us -> 67 us
  local copies, waits for them, and re-layouts: 2.58 us -> 1.78 us
    pallas_call x1, Pallas kernels: 70 us -> 67 us  [body(): pl.pallas_call(functools.partial(kernel, n_blk, n_dp), out_shape=jax.Shap...]
    reshape x0 -> x1, other arithmetic: none -> 1.3 us  [body(): jnp.where(live, partner_owner.T * rows + partner_row.T, -1)]
    select_n x1 -> x0, local copies, waits for them, and re-layouts: 0.8 us -> none  [body(): mine = jnp.where(live, partner_owner * rows + partner_row, -1)]
    unnamed x5 -> x3, local copies, waits for them, and re-layouts: 1.78 us -> 1.78 us
where the time goes in v3:
time: 71.7 us; the launch traced here: 71.4 us
  Pallas kernels  67 us (93%)
  local copies, waits for them, and re-layouts  1.78 us (2%)
  between operations  1.33 us (2%)
  other arithmetic  1.3 us (2%)
    pallas_call x1, Pallas kernels, body(): pl.pallas_call(functools.partial(kernel, n_blk, n_dp), out_shape=jax.Shap...  67 us
    unnamed x3, local copies, waits for them, and re-layouts  1.78 us

profile of v3, /device:TPU:1, one launch (start us, length us, event | category | flops | bytes accessed | tf_op | source)
XLA Modules:
  0.0 71.4 jit_solution(5673228623449802163)
XLA Ops:
  0.7 0.0 copy-start
  1.3 0.0 copy-done
  1.3 1.3 %fusion.theirs_ref = s32[1,4,256]{2,1,0:T(4,128)} fusion(s32[256,4]{0,1:T(4,128)} %param.11, s32[256,4]{0,1:T(4,128)} %param.10, s32[256]{0:T(256)S(1)} %copy-done), kind=kLoop, calls=%fused_computation.1 | loop fusion | flops 4096 | bytes 13312 | tf_op jit(solution)/shard_map/reshape | solution.py:305
  2.6 67.0 %shard_map.64 = bf16[256,768]{1,0:T(8,128)(2,1)} custom-call(f32[1]{0:T(128)S(6)} %copy.8.log_scale_ref, f32[1]{0:T(128)S(6)} %copy.9.bias_ref, bf16[256,768]{1,0:T(8,128)(2,1)} %x_ref.1, s32[1,4,256]{2,1,0:T(4,128)} %fusion.theirs_ref), custom_call_target="tpu_custom_call" | custom-call | tf_op jit(solution)/shard_map/pallas_call | solution.py:308
  69.7 1.8 %copy.10 = bf16[256,768]{1,0:T(8,128)(2,1)} copy(bf16[256,768]{1,0:T(8,128)(2,1)} %shard_map.64) | data formatting | bytes 786432
Async XLA Ops:
  0.7 0.7 copy-start

commit v4 on v3

--- a/solution.py
+++ b/solution.py
@@ -183,28 +183,27 @@
                 to_left(f, None, origin).start()
                 to_sib(f, origin).start()
 
-        f = slot(bi, zz, c)
-        passing = jnp.logical_and(valid, jnp.logical_and(m > 0, m < n_blk - 1))
-
-        @pl.when(passing)
-        def _():
-            arrived(f, None)
-
+        passing = jnp.logical_and(valid, jnp.logical_and(m % 2 == 1, m < n_blk - 1))
         for parity, send in ((1, to_right), (0, to_left)):
-            mine = jnp.logical_and(passing, m % 2 == parity)
-
-            @pl.when(jnp.logical_and(jnp.logical_and(mine, halves(zz)), d == far - 1))
-            def _():
-                send(f, 1 - parity, m * n_z + zz).start()
+            f = slot(blk_at(pos - d if parity else pos + d), zz, c)
+            index = (2 * d - parity) * n_z + zz
+
+            @pl.when(passing)
+            def _():
+                arrived(f, None)
+
+            @pl.when(jnp.logical_and(jnp.logical_and(passing, halves(zz)), d == far - 1))
+            def _():
+                send(f, 1 - parity, index).start()
 
             if far > 2:
-                @pl.when(jnp.logical_and(mine, d < far - 1))
-                def _():
-                    send(f, None, m * n_z + zz).start()
-
-        @pl.when(jnp.logical_and(passing, m > 0))
-        def _():
-            to_sib(f, m * n_z + zz).start()
+                @pl.when(jnp.logical_and(passing, d < far - 1))
+                def _():
+                    send(f, None, index).start()
+
+            @pl.when(passing)
+            def _():
+                to_sib(f, index).start()
 
         for step, k in ((1, 1), (-1, 0)):
             origin = z + step * t

time: 71.7 us -> 70.3 us (0.980)
  Pallas kernels: 67 us -> 65.7 us
    pallas_call x1, Pallas kernels: 67 us -> 65.7 us  [body(): pl.pallas_call(functools.partial(kernel, n_blk, n_dp), out_shape=jax.Shap...]
where the time goes in v4:
time: 70.3 us; the launch traced here: 70.1 us
  Pallas kernels  65.7 us (93%)
  local copies, waits for them, and re-layouts  1.78 us (3%)
  between operations  1.33 us (2%)
  other arithmetic  1.3 us (2%)
    pallas_call x1, Pallas kernels, body(): pl.pallas_call(functools.partial(kernel, n_blk, n_dp), out_shape=jax.Shap...  65.7 us
    unnamed x3, local copies, waits for them, and re-layouts  1.78 us

profile of v4, /device:TPU:1, one launch (start us, length us, event | category | flops | bytes accessed | tf_op | source)
XLA Modules:
  0.0 70.1 jit_solution(17868171434509064180)
XLA Ops:
  0.7 0.0 copy-start
  1.3 0.0 copy-done
  1.3 1.3 %fusion.theirs_ref = s32[1,4,256]{2,1,0:T(4,128)} fusion(s32[256,4]{0,1:T(4,128)} %param.11, s32[256,4]{0,1:T(4,128)} %param.10, s32[256]{0:T(256)S(1)} %copy-done), kind=kLoop, calls=%fused_computation.1 | loop fusion | flops 4096 | bytes 13312 | tf_op jit(solution)/shard_map/reshape | solution.py:304
  2.6 65.7 %shard_map.64 = bf16[256,768]{1,0:T(8,128)(2,1)} custom-call(f32[1]{0:T(128)S(6)} %copy.8.log_scale_ref, f32[1]{0:T(128)S(6)} %copy.9.bias_ref, bf16[256,768]{1,0:T(8,128)(2,1)} %x_ref.1, s32[1,4,256]{2,1,0:T(4,128)} %fusion.theirs_ref), custom_call_target="tpu_custom_call" | custom-call | tf_op jit(solution)/shard_map/pallas_call | solution.py:307
  68.3 1.8 %copy.10 = bf16[256,768]{1,0:T(8,128)(2,1)} copy(bf16[256,768]{1,0:T(8,128)(2,1)} %shard_map.64) | data formatting | bytes 786432
Async XLA Ops:
  0.7 0.7 copy-start
